TPU v7x, 32 devices: a whole 2x2x4 slice. The times are simulated.
32 devices in a mesh: seq: 8 (over y, x, core), slot: 4 (over z).
Axes of the slice: x: 2, y: 2, z: 4, core: 2. Of those that a mesh axis runs over, the one named last changes fastest.
Arguments:
- tokens: bfloat16 [8, 1024, 768], P('slot', 'seq'), may hold values from -6 to 6
- qkv_weight: bfloat16 [768, 2304], P(('seq', 'slot')), may hold values from -0.21875 to 0.21875
- query_bias: bfloat16 [768], P(('seq', 'slot')), may hold values from -3 to 3
- value_bias: bfloat16 [768], P(('seq', 'slot')), may hold values from -3 to 3
- out_weight: bfloat16 [768, 768], P(('seq', 'slot')), may hold values from -6 to 6
- out_bias: bfloat16 [768], P(('seq', 'slot')), may hold values from -3 to 3
- norm1_gain: bfloat16 [768], P(('seq', 'slot')), may hold values from 0.25 to 1.75
- norm1_shift: bfloat16 [768], P(('seq', 'slot')), may hold values from -2 to 2
- up_weight: bfloat16 [768, 3072], P(('seq', 'slot')), may hold values from -0.21875 to 0.21875
- up_bias: bfloat16 [3072], P(('seq', 'slot')), may hold values from -3 to 3
- down_weight: bfloat16 [3072, 768], P(('seq', 'slot')), may hold values from -0.109375 to 0.109375
- down_bias: bfloat16 [768], P(('seq', 'slot')), may hold values from -3 to 3
- norm2_gain: bfloat16 [768], P(('seq', 'slot')), may hold values from 0.25 to 1.75
- norm2_shift: bfloat16 [768], P(('seq', 'slot')), may hold values from -2 to 2
- slot_lengths: int32 [8], P('slot'), may hold values from 256 to 1024, as said below
- out_cotangent: bfloat16 [8, 1024, 768], P('slot', 'seq'), may hold values from -6 to 6
Outputs:
- layer_out: bfloat16 [8, 1024, 768], P('slot', 'seq')
- tokens_grad: bfloat16 [8, 1024, 768], P('slot', 'seq')
- qkv_weight_grad: float32 [768, 2304], P(('seq', 'slot'))
- query_bias_grad: float32 [768], P(('seq', 'slot'))
- value_bias_grad: float32 [768], P(('seq', 'slot'))
- out_weight_grad: float32 [768, 768], P(('seq', 'slot'))
- out_bias_grad: float32 [768], P(('seq', 'slot'))
- norm1_gain_grad: float32 [768], P(('seq', 'slot'))
- norm1_shift_grad: float32 [768], P(('seq', 'slot'))
- up_weight_grad: float32 [768, 3072], P(('seq', 'slot'))
- up_bias_grad: float32 [3072], P(('seq', 'slot'))
- down_weight_grad: float32 [3072, 768], P(('seq', 'slot'))
- down_bias_grad: float32 [768], P(('seq', 'slot'))
- norm2_gain_grad: float32 [768], P(('seq', 'slot'))
- norm2_shift_grad: float32 [768], P(('seq', 'slot'))
Inputs may be any that keep to these rules, and one draw needn't show every extreme that they name: `slot_lengths`: the valid tokens of each slot stand at its start; some slot is full and some holds 256 tokens.
All inputs are finite; a program needn't handle non-finite values.
Results may differ from a plain program's by a relative error of at most 0.015.
Values may be sent and summed in bfloat16 or wider, within the bound.
No kernel may reach another device: no remote copies, remote signals or barrier semaphores. Data moves between devices by JAX's collectives and lax.ppermute only.
A program may use at most 192 MiB of HBM per device.

v0:
```python
import jax
import jax.numpy as jnp
from jax import lax
from jax.sharding import PartitionSpec as P

HEADS = 12
NEG_FILL = -1e30
EPSILON = 1e-05


def norm_rows(resid, gain, shift):
    centre = resid - jnp.mean(resid, -1, keepdims=True)
    spread = jnp.mean(centre * centre, -1, keepdims=True)
    return centre * lax.rsqrt(spread + EPSILON) * gain + shift


def gelu_exact(inner_act):
    return jax.nn.gelu(inner_act, approximate=False)


def contract_rows(left, right):
    return lax.dot_general(
        left, right, (((0,), (0,)), ((), ())), preferred_element_type=jnp.float32
    )


def contract_last(left, right):
    return lax.dot_general(
        left, right, (((1,), (1,)), ((), ())), preferred_element_type=jnp.float32
    )


def split_heads(rows_in, head_count):
    return rows_in.reshape(
        rows_in.shape[0], rows_in.shape[1], head_count, rows_in.shape[2] // head_count
    )


def take_block(whole, position, block_size, axis_dim):
    return lax.dynamic_slice_in_dim(whole, position * block_size, block_size, axis_dim)


def masked_scores(queries, key_rows, key_start, slot_lengths):
    scores = jnp.einsum("sqhd,skhd->shqk", queries, key_rows, preferred_element_type=jnp.float32)
    key_places = key_start + jnp.arange(key_rows.shape[1])
    live_keys = key_places[None, :] < slot_lengths[:, None]
    return jnp.where(live_keys[:, None, None, :], scores, NEG_FILL)


def log_totals(queries, key_all, slot_lengths, block_size, head_count):
    block_count = key_all.shape[1] // block_size
    stat_shape = (queries.shape[0], head_count, queries.shape[1])

    def log_step_fn(carried, position):
        running_max, running_sum = carried
        key_rows = split_heads(take_block(key_all, position, block_size, 1), head_count)
        scores = masked_scores(queries, key_rows, position * block_size, slot_lengths)
        new_max = jnp.maximum(running_max, jnp.max(scores, -1))
        running_sum = running_sum * jnp.exp(running_max - new_max) + jnp.sum(
            jnp.exp(scores - new_max[..., None]), -1
        )
        return ((new_max, running_sum), None)

    start_state = (jnp.full(stat_shape, NEG_FILL, jnp.float32), jnp.zeros(stat_shape, jnp.float32))
    (running_max, running_sum), _ = lax.scan(log_step_fn, start_state, jnp.arange(block_count))
    return running_max + jnp.log(running_sum)


def attend(queries, key_all, value_all, slot_lengths, logsum, block_size, head_count):
    block_count = key_all.shape[1] // block_size

    def attend_step_fn(context, position):
        key_rows = split_heads(take_block(key_all, position, block_size, 1), head_count)
        value_rows = split_heads(take_block(value_all, position, block_size, 1), head_count)
        scores = masked_scores(queries, key_rows, position * block_size, slot_lengths)
        weights_low = jnp.exp(scores - logsum[..., None]).astype(jnp.bfloat16)
        return (
            context
            + jnp.einsum(
                "shqk,skhd->sqhd", weights_low, value_rows, preferred_element_type=jnp.float32
            ),
            None,
        )

    context, _ = lax.scan(
        attend_step_fn, jnp.zeros(queries.shape, jnp.float32), jnp.arange(block_count)
    )
    return context


def prob_grad_totals(
    queries, d_context, key_all, value_all, slot_lengths, logsum, block_size, head_count
):
    block_count = key_all.shape[1] // block_size

    def prob_step_fn(prob_delta, position):
        key_rows = split_heads(take_block(key_all, position, block_size, 1), head_count)
        value_rows = split_heads(take_block(value_all, position, block_size, 1), head_count)
        scores = masked_scores(queries, key_rows, position * block_size, slot_lengths)
        softmax_rows = jnp.exp(scores - logsum[..., None])
        d_probs = jnp.einsum(
            "sqhd,skhd->shqk", d_context, value_rows, preferred_element_type=jnp.float32
        )
        return (prob_delta + jnp.sum(softmax_rows * d_probs, -1), None)

    prob_delta, _ = lax.scan(
        prob_step_fn, jnp.zeros(logsum.shape, jnp.float32), jnp.arange(block_count)
    )
    return prob_delta


def key_side(
    queries, d_context, key_all, value_all, slot_lengths, logsum, prob_delta, block_size, head_count
):
    block_count = key_all.shape[1] // block_size

    def key_step_fn(d_query, position):
        key_rows = split_heads(take_block(key_all, position, block_size, 1), head_count)
        value_rows = split_heads(take_block(value_all, position, block_size, 1), head_count)
        scores = masked_scores(queries, key_rows, position * block_size, slot_lengths)
        softmax_rows = jnp.exp(scores - logsum[..., None])
        d_probs = jnp.einsum(
            "sqhd,skhd->shqk", d_context, value_rows, preferred_element_type=jnp.float32
        )
        d_scores = (softmax_rows * (d_probs - prob_delta[..., None])).astype(jnp.bfloat16)
        d_query = d_query + jnp.einsum(
            "shqk,skhd->sqhd", d_scores, key_rows, preferred_element_type=jnp.float32
        )
        d_key_rows = jnp.einsum(
            "shqk,sqhd->skhd", d_scores, queries, preferred_element_type=jnp.float32
        )
        d_value_rows = jnp.einsum(
            "shqk,sqhd->skhd",
            softmax_rows.astype(jnp.bfloat16),
            d_context,
            preferred_element_type=jnp.float32,
        )
        return (d_query, (d_key_rows, d_value_rows))

    return lax.scan(key_step_fn, jnp.zeros(queries.shape, jnp.float32), jnp.arange(block_count))


def body(
    tokens,
    qkv_weight,
    query_bias,
    value_bias,
    out_weight,
    out_bias,
    norm1_gain,
    norm1_shift,
    up_weight,
    up_bias,
    down_weight,
    down_bias,
    norm2_gain,
    norm2_shift,
    slot_lengths,
    out_cotangent,
):
    slot_count, row_count, model_width = tokens.shape
    head_count = HEADS
    flat_rows = tokens.reshape(slot_count * row_count, model_width)
    attn_set = (
        lax.all_gather(qkv_weight, ("seq", "slot"), axis=0, tiled=True),
        lax.all_gather(out_weight, ("seq", "slot"), axis=0, tiled=True),
        lax.all_gather(query_bias, ("seq", "slot"), axis=0, tiled=True),
        lax.all_gather(value_bias, ("seq", "slot"), axis=0, tiled=True),
        lax.all_gather(out_bias, ("seq", "slot"), axis=0, tiled=True),
        lax.all_gather(norm1_gain, ("seq", "slot"), axis=0, tiled=True),
        lax.all_gather(norm1_shift, ("seq", "slot"), axis=0, tiled=True),
    )
    qkv_full, out_full, query_shift, value_shift, out_shift, gain_one, shift_one = attn_set
    mixed = jnp.dot(flat_rows, qkv_full, preferred_element_type=jnp.float32)
    queries = ((mixed[:, :model_width] + query_shift.astype(jnp.float32)) * 0.125).astype(
        jnp.bfloat16
    )
    queries = split_heads(queries.reshape(slot_count, row_count, model_width), head_count)
    keys_own = (
        mixed[:, model_width : 2 * model_width]
        .astype(jnp.bfloat16)
        .reshape(slot_count, row_count, model_width)
    )
    values_own = (
        (mixed[:, 2 * model_width :] + value_shift.astype(jnp.float32))
        .astype(jnp.bfloat16)
        .reshape(slot_count, row_count, model_width)
    )
    key_all, value_all = (
        lax.all_gather(keys_own, "seq", axis=1, tiled=True),
        lax.all_gather(values_own, "seq", axis=1, tiled=True),
    )
    length_all = key_all.shape[1]
    block_size = min(512, length_all)
    logsum = log_totals(queries, key_all, slot_lengths, block_size, head_count)
    context = attend(
        queries, key_all, value_all, slot_lengths, logsum, block_size, head_count
    ).astype(jnp.bfloat16)
    context_flat = context.reshape(slot_count * row_count, model_width)
    attn_out = jnp.dot(
        context_flat, out_full, preferred_element_type=jnp.float32
    ) + out_shift.astype(jnp.float32)
    resid_one = flat_rows.astype(jnp.float32) + attn_out
    hidden_one = norm_rows(resid_one, gain_one.astype(jnp.float32), shift_one.astype(jnp.float32))
    hidden_low = hidden_one.astype(jnp.bfloat16)
    ffn_set = (
        lax.all_gather(up_weight, ("seq", "slot"), axis=0, tiled=True),
        lax.all_gather(down_weight, ("seq", "slot"), axis=0, tiled=True),
        lax.all_gather(up_bias, ("seq", "slot"), axis=0, tiled=True),
        lax.all_gather(down_bias, ("seq", "slot"), axis=0, tiled=True),
        lax.all_gather(norm2_gain, ("seq", "slot"), axis=0, tiled=True),
        lax.all_gather(norm2_shift, ("seq", "slot"), axis=0, tiled=True),
    )
    up_full, down_full, up_shift, down_shift, gain_two, shift_two = ffn_set
    inner_act = jnp.dot(hidden_low, up_full, preferred_element_type=jnp.float32) + up_shift.astype(
        jnp.float32
    )
    activated = gelu_exact(inner_act).astype(jnp.bfloat16)
    ffn_out = jnp.dot(activated, down_full, preferred_element_type=jnp.float32) + down_shift.astype(
        jnp.float32
    )
    resid_two = hidden_one + ffn_out
    layer_out = norm_rows(resid_two, gain_two.astype(jnp.float32), shift_two.astype(jnp.float32))
    layer_out = layer_out.astype(jnp.bfloat16).reshape(slot_count, row_count, model_width)
    qkv_back, out_back, _, _, _, gain_one_back, shift_one_back = (
        lax.all_gather(qkv_weight, ("seq", "slot"), axis=0, tiled=True),
        lax.all_gather(out_weight, ("seq", "slot"), axis=0, tiled=True),
        lax.all_gather(query_bias, ("seq", "slot"), axis=0, tiled=True),
        lax.all_gather(value_bias, ("seq", "slot"), axis=0, tiled=True),
        lax.all_gather(out_bias, ("seq", "slot"), axis=0, tiled=True),
        lax.all_gather(norm1_gain, ("seq", "slot"), axis=0, tiled=True),
        lax.all_gather(norm1_shift, ("seq", "slot"), axis=0, tiled=True),
    )
    up_back, down_back, _, _, gain_two_back, shift_two_back = (
        lax.all_gather(up_weight, ("seq", "slot"), axis=0, tiled=True),
        lax.all_gather(down_weight, ("seq", "slot"), axis=0, tiled=True),
        lax.all_gather(up_bias, ("seq", "slot"), axis=0, tiled=True),
        lax.all_gather(down_bias, ("seq", "slot"), axis=0, tiled=True),
        lax.all_gather(norm2_gain, ("seq", "slot"), axis=0, tiled=True),
        lax.all_gather(norm2_shift, ("seq", "slot"), axis=0, tiled=True),
    )
    positions = lax.axis_index("seq") * row_count + jnp.arange(row_count)
    live_rows = (positions[None, :] < slot_lengths[:, None]).astype(jnp.float32)
    cotangent = (out_cotangent.astype(jnp.float32) * live_rows[:, :, None]).reshape(
        slot_count * row_count, model_width
    )
    _, norm_back_two = jax.vjp(
        norm_rows, resid_two, gain_two_back.astype(jnp.float32), shift_two_back.astype(jnp.float32)
    )
    d_resid_two, d_gain_two, d_shift_two = norm_back_two(cotangent)
    d_ffn = d_resid_two.astype(jnp.bfloat16)
    d_down = contract_rows(activated, d_ffn)
    d_down_shift = jnp.sum(d_ffn.astype(jnp.float32), 0)
    d_activated = contract_last(d_ffn, down_back)
    _, gelu_back = jax.vjp(gelu_exact, inner_act)
    d_inner = gelu_back(d_activated)[0].astype(jnp.bfloat16)
    d_up = contract_rows(hidden_low, d_inner)
    d_up_shift = jnp.sum(d_inner.astype(jnp.float32), 0)
    d_hidden = contract_last(d_inner, up_back) + d_resid_two
    _, norm_back_one = jax.vjp(
        norm_rows, resid_one, gain_one_back.astype(jnp.float32), shift_one_back.astype(jnp.float32)
    )
    d_resid_one, d_gain_one, d_shift_one = norm_back_one(d_hidden)
    d_attn = d_resid_one.astype(jnp.bfloat16)
    d_out = contract_rows(context_flat, d_attn)
    d_out_shift = jnp.sum(d_attn.astype(jnp.float32), 0)
    d_context = contract_last(d_attn, out_back).astype(jnp.bfloat16)
    d_context = split_heads(d_context.reshape(slot_count, row_count, model_width), head_count)
    prob_delta = prob_grad_totals(
        queries, d_context, key_all, value_all, slot_lengths, logsum, block_size, head_count
    )
    d_query, key_parts = key_side(
        queries,
        d_context,
        key_all,
        value_all,
        slot_lengths,
        logsum,
        prob_delta,
        block_size,
        head_count,
    )
    d_key_part = jnp.moveaxis(key_parts[0], 0, 1).reshape(slot_count, length_all, model_width)
    d_value_part = jnp.moveaxis(key_parts[1], 0, 1).reshape(slot_count, length_all, model_width)
    d_key_sum, d_value_sum = (
        lax.psum_scatter(
            d_key_part.astype(jnp.bfloat16), "seq", scatter_dimension=1, tiled=True
        ).astype(jnp.float32),
        lax.psum_scatter(
            d_value_part.astype(jnp.bfloat16), "seq", scatter_dimension=1, tiled=True
        ).astype(jnp.float32),
    )
    d_query_pre = d_query.astype(jnp.bfloat16).reshape(
        slot_count * row_count, model_width
    ) * jnp.asarray(0.125, jnp.bfloat16)
    d_key_low = d_key_sum.astype(jnp.bfloat16).reshape(slot_count * row_count, model_width)
    d_value_low = d_value_sum.astype(jnp.bfloat16).reshape(slot_count * row_count, model_width)
    d_mixed = jnp.concatenate([d_query_pre, d_key_low, d_value_low], 1)
    d_qkv = contract_rows(flat_rows, d_mixed)
    d_query_shift = jnp.sum(d_query_pre.astype(jnp.float32), 0)
    d_value_shift = jnp.sum(d_value_low.astype(jnp.float32), 0)
    tokens_grad = (
        (d_resid_one + contract_last(d_mixed, qkv_back))
        .astype(jnp.bfloat16)
        .reshape(slot_count, row_count, model_width)
    )
    attn_sums = (
        lax.psum_scatter(d_qkv, ("seq", "slot"), scatter_dimension=0, tiled=True),
        lax.psum_scatter(d_out, ("seq", "slot"), scatter_dimension=0, tiled=True),
        lax.psum_scatter(d_query_shift, ("seq", "slot"), scatter_dimension=0, tiled=True),
        lax.psum_scatter(d_value_shift, ("seq", "slot"), scatter_dimension=0, tiled=True),
        lax.psum_scatter(d_out_shift, ("seq", "slot"), scatter_dimension=0, tiled=True),
        lax.psum_scatter(d_gain_one, ("seq", "slot"), scatter_dimension=0, tiled=True),
        lax.psum_scatter(d_shift_one, ("seq", "slot"), scatter_dimension=0, tiled=True),
    )
    ffn_sums = (
        lax.psum_scatter(d_up, ("seq", "slot"), scatter_dimension=0, tiled=True),
        lax.psum_scatter(d_down, ("seq", "slot"), scatter_dimension=0, tiled=True),
        lax.psum_scatter(d_up_shift, ("seq", "slot"), scatter_dimension=0, tiled=True),
        lax.psum_scatter(d_down_shift, ("seq", "slot"), scatter_dimension=0, tiled=True),
        lax.psum_scatter(d_gain_two, ("seq", "slot"), scatter_dimension=0, tiled=True),
        lax.psum_scatter(d_shift_two, ("seq", "slot"), scatter_dimension=0, tiled=True),
    )
    return (
        layer_out,
        tokens_grad,
        attn_sums[0],
        attn_sums[2],
        attn_sums[3],
        attn_sums[1],
        attn_sums[4],
        attn_sums[5],
        attn_sums[6],
        ffn_sums[0],
        ffn_sums[2],
        ffn_sums[1],
        ffn_sums[3],
        ffn_sums[4],
        ffn_sums[5],
    )


def solution(mesh):
    return jax.shard_map(
        body,
        mesh=mesh,
        in_specs=(
            P("slot", "seq", None),
            P(("seq", "slot"), None),
            P(("seq", "slot")),
            P(("seq", "slot")),
            P(("seq", "slot"), None),
            P(("seq", "slot")),
            P(("seq", "slot")),
            P(("seq", "slot")),
            P(("seq", "slot"), None),
            P(("seq", "slot")),
            P(("seq", "slot"), None),
            P(("seq", "slot")),
            P(("seq", "slot")),
            P(("seq", "slot")),
            P("slot"),
            P("slot", "seq", None),
        ),
        out_specs=(
            P("slot", "seq", None),
            P("slot", "seq", None),
            P(("seq", "slot"), None),
            P(("seq", "slot")),
            P(("seq", "slot")),
            P(("seq", "slot"), None),
            P(("seq", "slot")),
            P(("seq", "slot")),
            P(("seq", "slot")),
            P(("seq", "slot"), None),
            P(("seq", "slot")),
            P(("seq", "slot"), None),
            P(("seq", "slot")),
            P(("seq", "slot")),
            P(("seq", "slot")),
        ),
        check_vma=False,
    )
```

profile of v0, /device:TPU:0, one launch (start us, length us, event | category | flops | bytes accessed | tf_op | source)
XLA Modules:
  0.0 1040.6 jit_solution(14820919905901474009)
XLA Ops:
  8.0 65.6 %all-gather.7.cloned.1.call-done = bf16[768,2304]{1,0:T(8,128)(2,1)} async-done(((bf16[24,2304]{1,0:T(8,128)(2,1)}), bf16[768,2304]{1,0:T(8,128)(2,1)}) %all-gather.7.cloned.1.call-update) | async-done | bytes 3538960 | tf_op jit(solution)/shard_map/all_gather | solution.py:165
  73.6 3.3 fusion.54
  80.2 39.2 %all-reduce.19 = (bf16[3072]{0:T(1024)(128)(2,1)S(1)}, bf16[768]{0:T(1024)(128)(2,1)}, bf16[768]{0:T(1024)(128)(2,1)S(1)}, bf16[768]{0:T(1024)(128)(2,1)S(1)}, b...) all-reduce(bf16[3072]{0:T(1024)(128)(2,1)S(1)} %dynamic-update-slic, ...), channel_id=1, replica_groups=mesh['seq'=8,'slot'=4] {'seq','slot'}, use_global_device_ids=true, to_apply=%add.5 | all-reduce | flops 9216 | bytes 36864
  122.8 1.6 fusion.41
  127.0 1.3 convert_element_type.135
  132.4 21.4 %while.50 = (s32[]{:T(128)}, f32[2,12,128]{2,1,0:T(8,128)S(1)}, f32[2,12,128]{2,1,0:T(8,128)S(1)}, s32[2]{0:T(128)S(1)}, s32[2]{0:T(128)S(1)}, /*index=5*/bf16[2...) while((s32[]{:T(128)}, f32[2,12,128]{2,1,0:T(8,128)S(1)}, ...), condition=%wide.region_3.4_spmd.clone, body=%wide.region_0.3_spmd.clone.sunk | while | flops 209207808 | bytes 17861824 | solution.py:65
  133.7 1.5 constant_dynamic-slice_fusion.11
  135.3 4.1 bitcast_reduce_fusion.2
  139.4 3.9 fusion.121
  144.5 1.5 constant_dynamic-slice_fusion.11
  146.1 4.1 bitcast_reduce_fusion.2
  150.2 3.5 fusion.121
  154.5 17.4 %while.51 = (s32[]{:T(128)}, f32[2,128,12,64]{1,3,2,0:T(8,128)}, s32[2]{0:T(128)}, bf16[2,1024,768]{1,2,0:T(8,128)(2,1)}, s32[2]{0:T(128)}, /*index=5*/bf16[2,10...) while((s32[]{:T(128)}, f32[2,128,12,64]{1,3,2,0:T(8,128)}, ...), condition=%wide.region_5.6_spmd.clone, body=%wide.region_4.5_spmd.clone.sunk | while | flops 407766528 | bytes 11421957 | solution.py:85
  156.4 2.1 constant_dynamic-slice_fusion.12
  159.1 3.8 fusion.126
  164.8 2.1 constant_dynamic-slice_fusion.12
  167.6 4.2 fusion.126
  173.5 37.2 %all-gather.13.cloned.1.call-done = bf16[768,768]{1,0:T(8,128)(2,1)} async-done(((bf16[24,768]{1,0:T(8,128)(2,1)}), bf16[768,768]{1,0:T(8,128)(2,1)}) %all-gather.13.cloned.1.call-update) | async-done | bytes 1179664 | tf_op jit(solution)/shard_map/all_gather | solution.py:166
  210.6 2.0 fusion.50
  212.9 62.9 %all-gather.15.cloned.1.call-done = bf16[768,3072]{1,0:T(8,128)(2,1)} async-done(((bf16[24,3072]{1,0:T(8,128)(2,1)}), bf16[768,3072]{1,0:T(8,128)(2,1)}) %all-gather.15.cloned.1.call-update) | async-done | bytes 4718608 | tf_op jit(solution)/shard_map/all_gather | solution.py:207
  275.8 11.5 %multiply_convert_fusion.1 = (bf16[256,3072]{1,0:T(8,128)(2,1)S(1)}, f32[256,3072]{1,0:T(8,128)}, f32[256,3072]{1,0:T(8,128)}) fusion(f32[3072]{0:T(1024)S(1)} %copy-done.48, bf16[768,3072]{1,0:T(8,128)(2,1)} %all-gather.15.cloned.1.call-done, f32[256,768]{1,0:T(8,128)S(1)} %get-tuple-element.609, f32[768]{0:T(1024)S(1)} %copy-done.38, ...), kind=kOutput, calls=%fused_computation.53 | convolution fusion | flops 1260847104 | bytes 13389824 | tf_op jit(solution)/shard_map/dot_general | solution.py:215
  287.3 53.1 %all-gather.17.cloned.1.call-done = bf16[3072,768]{1,0:T(8,128)(2,1)} async-done(((bf16[96,768]{1,0:T(8,128)(2,1)}), bf16[3072,768]{1,0:T(8,128)(2,1)}) %all-gather.17.cloned.1.call-update) | async-done | bytes 4718608 | tf_op jit(solution)/shard_map/all_gather | solution.py:208
  340.5 4.0 fusion.51
  347.5 2.7 convert_reduce_fusion
  350.3 2.3 multiply_reduce_fusion.1
  356.3 13.5 %while.52 = (s32[]{:T(128)}, f32[2,12,128]{2,1,0:T(8,128)S(1)}, s32[2]{0:T(128)S(1)}, s32[2]{0:T(128)S(1)}, bf16[2,1024,768]{1,2,0:T(8,128)(2,1)}, /*index=5*/bf...) while((s32[]{:T(128)}, f32[2,12,128]{2,1,0:T(8,128)S(1)}, ...), condition=%wide.region_16.17_spmd.clone, body=%wide.region_14.16_spmd.clone.sunk | while | flops 408949248 | bytes 22874320 | solution.py:106
  357.6 2.1 constant_dynamic-slice_fusion.13
  360.8 2.2 multiply_reduce_fusion.7
  364.3 2.1 constant_dynamic-slice_fusion.13
  367.5 2.2 multiply_reduce_fusion.7
  369.8 37.0 %while.53 = (s32[]{:T(128)}, f32[2,128,12,64]{1,3,2,0:T(8,128)}, bf16[2,2,512,12,64]{2,4,3,1,0:T(8,128)(2,1)}, bf16[2,2,512,12,64]{2,4,3,1,0:T(8,128)(2,1)}, s32...) while((s32[]{:T(128)}, f32[2,128,12,64]{1,3,2,0:T(8,128)}, ...), condition=%wide.region_18.19_spmd.clone, body=%wide.region_17.18_spmd.clone.sunk | while | flops 1019610624 | bytes 108679904 | solution.py:140
  371.3 2.1 constant_dynamic-slice_fusion.14
  374.7 3.9 multiply_convert_fusion.3
  378.6 2.4 bitcast_dynamic-update-slice_fusion.7
  381.0 3.2 fusion.143
  384.3 3.9 bitcast_dynamic-update-slice_fusion.8
  389.5 2.1 constant_dynamic-slice_fusion.14
  392.9 3.9 multiply_convert_fusion.3
  396.8 2.5 bitcast_dynamic-update-slice_fusion.7
  399.3 3.4 fusion.143
  402.8 3.9 bitcast_dynamic-update-slice_fusion.8
  406.8 5.1 copy.69
  411.9 3.9 convert_element_type.152
  415.8 7.6 copy.74
  423.5 2.3 copy.84
  426.1 5.1 copy.71
  431.2 3.9 convert_element_type.155
  435.1 7.7 copy.76
  442.8 2.3 copy.86
  446.4 1.9 fusion.36
  448.4 5.2 fusion.44
  453.7 1.3 copy-done.16
  455.1 5.1 fusion.55
  462.0 8.3 reduce-scatter.19.cloned.1.call-done
  471.9 47.9 %reduce-scatter.21.cloned.1.call-done = bf16[128,1536]{1,0:T(8,128)(2,1)} async-done(((bf16[1024,1536]{1,0:T(8,128)(2,1)}), bf16[128,1536]{1,0:T(8,128)(2,1)}) %reduce-scatter.21.cloned.1.call-update) | async-done | bytes 393232
  521.5 3.9 convolution_bitcast_fusion.1
  525.5 8.0 copy.78
  534.2 2.3 copy.77
  537.7 41.0 %all-reduce.18 = (f32[768]{0:T(1024)}, f32[768]{0:T(1024)}, f32[768]{0:T(1024)}, f32[768]{0:T(1024)}, f32[768]{0:T(1024)}, /*index=5*/f32[3072]{0:T(1024)}, f32[768]{0:T(1024)}, f32[768]{0:T(1024)}, f32[768]{0:T(1024)S(1)}) all-reduce(f32[768]{0:T(1024)} %reduce_sum.185, ...), channel_id=5, replica_groups=mesh['seq'=8,'slot'=4] {'seq','slot'}, use_global_device_ids=true, to_apply=%region_23.24.clone | all-reduce | flops 9216 | bytes 73728
  589.3 3.4 fusion.30
  592.7 32.7 %reduce-scatter.13.cloned.1.call-done = f32[24,768]{1,0:T(8,128)} async-done(((f32[768,768]{1,0:T(8,128)}), f32[24,768]{1,0:T(8,128)}) %reduce-scatter.13.cloned.1.call-update) | async-done | bytes 73744 | tf_op jit(solution)/shard_map/reduce_scatter | solution.py:309
  625.5 141.6 %reduce-scatter.15.cloned.1.call-done = f32[24,3072]{1,0:T(8,128)} async-done(((f32[768,3072]{1,0:T(8,128)}), f32[24,3072]{1,0:T(8,128)}) %reduce-scatter.15.cloned.1.call-update) | async-done | bytes 294928 | tf_op jit(solution)/shard_map/reduce_scatter | solution.py:317
  767.1 141.6 %reduce-scatter.17.cloned.1.call-done = f32[96,768]{1,0:T(8,128)} async-done(((f32[3072,768]{1,0:T(8,128)}), f32[96,768]{1,0:T(8,128)}) %reduce-scatter.17.cloned.1.call-update) | async-done | bytes 294928 | tf_op jit(solution)/shard_map/reduce_scatter | solution.py:318
  908.7 124.6 %reduce-scatter.23.cloned.1.call-done = f32[24,2304]{1,0:T(8,128)} async-done(((f32[768,2304]{1,0:T(8,128)}), f32[24,2304]{1,0:T(8,128)}) %reduce-scatter.23.cloned.1.call-update) | async-done | bytes 221200
  (315 shorter events, 55.0 us)
Async XLA Ops:
  7.2 66.4 %all-gather.7.cloned.1.call-start = ((), (), s32[]{:S(2)}) async-start(), calls=%async_computation.6 | async-start | bytes 3649536 | tf_op jit(solution)/shard_map/all_gather | solution.py:165
  7.9 124.5 %all-gather.11.cloned.1.call-start = ((), (), s32[]{:S(2)}) async-start(), calls=%async_computation.8 | async-start | bytes 3538944 | tf_op jit(solution)/shard_map/all_gather | solution.py:190
  73.6 4.4 copy-start.51
  73.6 4.7 copy-start.52
  73.6 4.9 copy-start.53
  73.6 5.2 copy-start.54
  73.6 5.4 copy-start.55
  73.6 5.6 copy-start.56
  73.6 5.8 copy-start.57
  73.6 6.1 copy-start.58
  73.6 6.3 copy-start.59
  76.9 45.8 %copy-start.31 = (s32[2]{0:T(128)S(1)}, s32[2]{0:T(128)}, u32[]{:S(2)}) copy-start(s32[2]{0:T(128)} %param.38) | copy-start | bytes 28
  76.9 45.9 %copy-start.30 = (bf16[2,128,768]{2,1,0:T(8,128)(2,1)S(1)}, bf16[2,128,768]{2,1,0:T(8,128)(2,1)}, u32[]{:S(2)}) copy-start(bf16[2,128,768]{2,1,0:T(8,128)(2,1)} %param.39) | copy-start | bytes 1179652
  77.9 76.0 %all-gather.9.cloned.1.call-start = ((), (), s32[]{:S(2)}) async-start(), calls=%async_computation.7 | async-start | bytes 3538944 | tf_op jit(solution)/shard_map/all_gather | solution.py:191
  120.5 90.2 %all-gather.13.cloned.1.call-start = ((), (), s32[]{:S(2)}) async-start(), calls=%async_computation.9 | async-start | bytes 1216512 | tf_op jit(solution)/shard_map/all_gather | solution.py:166
  121.0 154.8 %all-gather.15.cloned.1.call-start = ((), (), s32[]{:S(2)}) async-start(), calls=%async_computation.10 | async-start | bytes 4866048 | tf_op jit(solution)/shard_map/all_gather | solution.py:207
  121.6 218.8 %all-gather.17.cloned.1.call-start = ((), (), s32[]{:S(2)}) async-start(), calls=%async_computation.11 | async-start | bytes 4866048 | tf_op jit(solution)/shard_map/all_gather | solution.py:208
  122.2 348.1 %reduce-scatter.19.cloned.1.call-start = ((), (), s32[]{:S(2)}) async-start(), calls=%async_computation.15 | async-start | bytes 3538944
  171.8 104.0 %copy-start.36 = (f32[768]{0:T(1024)S(1)}, f32[768]{0:T(1024)}, u32[]{:S(2)}) copy-start(f32[768]{0:T(1024)} %convert_element_type.134) | copy-start | bytes 9220
  171.8 104.0 %copy-start.38 = (f32[768]{0:T(1024)S(1)}, f32[768]{0:T(1024)}, u32[]{:S(2)}) copy-start(f32[768]{0:T(1024)} %convert_element_type.135) | copy-start | bytes 9220
  171.8 104.0 %copy-start.48 = (f32[3072]{0:T(1024)S(1)}, f32[3072]{0:T(1024)}, u32[]{:S(2)}) copy-start(f32[3072]{0:T(1024)} %convert_element_type.137) | copy-start | bytes 36868
  173.4 39.4 %copy-start.23 = (bf16[2,128,12,64]{1,0,3,2:T(2,128)(2,1)}, bf16[2,128,12,64]{1,0,3,2:T(2,128)(2,1)S(1)}, u32[]{:S(2)}) copy-start(bf16[2,128,12,64]{1,0,3,2:T(2,128)(2,1)S(1)} %copy.62) | copy-start | bytes 1179652
  212.6 140.0 %copy-start.7 = (f32[256,768]{1,0:T(8,128)}, f32[256,768]{1,0:T(8,128)S(1)}, u32[]{:S(2)}) copy-start(f32[256,768]{1,0:T(8,128)S(1)} %get-tuple-element.609) | copy-start | bytes 2359300
  212.6 140.0 %copy-start.41 = (f32[256]{0:T(256)}, f32[256]{0:T(256)S(1)}, u32[]{:S(2)}) copy-start(f32[256]{0:T(256)S(1)} %broadcast_multiply_fusion.1) | copy-start | bytes 3076
  212.9 139.8 %copy-start.46 = (f32[256]{0:T(256)}, f32[256]{0:T(256)S(1)}, u32[]{:S(2)}) copy-start(f32[256]{0:T(256)S(1)} %fusion.42) | copy-start | bytes 3076
  212.9 127.5 %copy-start.49 = (f32[768]{0:T(1024)S(1)}, f32[768]{0:T(1024)}, u32[]{:S(2)}) copy-start(f32[768]{0:T(1024)} %convert_element_type.139) | copy-start | bytes 9220
  287.3 57.1 %copy-start.15 = (bf16[256,3072]{1,0:T(8,128)(2,1)}, bf16[256,3072]{1,0:T(8,128)(2,1)S(1)}, u32[]{:S(2)}) copy-start(bf16[256,3072]{1,0:T(8,128)(2,1)S(1)} %get-tuple-element.593) | copy-start | bytes 4718596
  340.4 7.1 slice-start.2
  340.4 4.3 copy-start.6
  340.4 4.3 copy-start.40
  340.4 5.2 copy-start.43
  340.4 7.0 slice-start.3
  346.7 3.5 slice-start
  370.0 3.4 copy-start.3
  370.0 3.4 copy-start.18
  370.1 4.6 copy-start.34
  374.6 4.0 copy-start
  374.7 3.9 copy-start.28
  384.2 3.9 copy-start.4
  384.2 3.9 copy-start.19
  384.2 3.9 copy-start.35
  384.2 3.9 copy-start.61
  388.2 3.4 copy-start.3
  388.2 3.4 copy-start.18
  388.2 4.6 copy-start.34
  392.8 4.0 copy-start
  392.9 3.9 copy-start.28
  399.3 3.6 copy-start.1
  399.3 3.6 copy-start.29
  402.8 3.9 copy-start.4
  402.8 3.9 copy-start.19
  402.8 3.9 copy-start.35
  402.8 3.9 copy-start.61
  425.8 94.0 %reduce-scatter.21.cloned.1.call-start = ((), (), s32[]{:S(2)}) async-start(), calls=%async_computation.16 | async-start | bytes 3538944
  445.2 180.3 %reduce-scatter.13.cloned.1.call-start = ((), (), s32[]{:S(2)}) async-start(), calls=%async_computation.12 | async-start | bytes 2433024 | tf_op jit(solution)/shard_map/reduce_scatter | solution.py:309
  448.3 318.8 %reduce-scatter.15.cloned.1.call-start = ((), (), s32[]{:S(2)}) async-start(), calls=%async_computation.13 | async-start | bytes 9732096 | tf_op jit(solution)/shard_map/reduce_scatter | solution.py:317
  453.7 455.1 %reduce-scatter.17.cloned.1.call-start = ((), (), s32[]{:S(2)}) async-start(), calls=%async_computation.14 | async-start | bytes 9732096 | tf_op jit(solution)/shard_map/reduce_scatter | solution.py:318
  460.2 573.0 %reduce-scatter.23.cloned.1.call-start = ((), (), s32[]{:S(2)}) async-start(), calls=%async_computation.17 | async-start | bytes 7299072
  461.5 60.0 %copy-start.22 = (bf16[2,128,768]{2,1,0:T(8,128)(2,1)S(1)}, bf16[2,128,768]{2,1,0:T(8,128)(2,1)}, u32[]{:S(2)}) copy-start(bf16[2,128,768]{2,1,0:T(8,128)(2,1)} %param.24) | copy-start | bytes 1179652
  520.9 4.6 copy-start.10
  521.5 3.9 copy-start.13
  533.5 4.2 copy-start.44
  533.5 4.2 copy-start.45
  533.5 55.8 %copy-start.9 = (bf16[768,2304]{1,0:T(8,128)(2,1)S(1)}, bf16[768,2304]{1,0:T(8,128)(2,1)}, u32[]{:S(2)}) copy-start(bf16[768,2304]{1,0:T(8,128)(2,1)} %all-gather.7.cloned.1.call-done) | copy-start | bytes 10616836
  (30 other events, 74.0 us)
Sparse Core Ops, SparseCore 0:
  10.8 62.7 all-gather.6
  78.1 31.7 all-gather.10
  120.6 33.3 all-gather.8
  156.6 54.0 all-gather.12
  213.3 62.5 all-gather.14
  278.5 61.8 all-gather.16
  425.9 44.3 reduce-scatter.18
  473.7 46.0 reduce-scatter.20
  525.6 99.7 reduce-scatter.12
  631.8 135.2 reduce-scatter.14
  773.6 135.1 reduce-scatter.16
  914.8 118.4 reduce-scatter.22
where the time goes:
time: 1050 us; the launch traced here: 1040 us
  waiting for transfers between devices  718 us (68%)
  matrix products  97.6 us (9%)
  local copies, waits for them, and re-layouts  96.6 us (9%)
  blocking collectives  80.2 us (8%)
  other arithmetic  25.5 us (2%)
  between operations  15.5 us (1%)
    unnamed x15, waiting for transfers between devices  183 us
    reduce_scatter x1, waiting for transfers between devices, body(): lax.psum_scatter(d_down, ('seq', 'slot'), scatter_dimension=0, tiled=True)  142 us
    reduce_scatter x1, waiting for transfers between devices, body(): lax.psum_scatter(d_up, ('seq', 'slot'), scatter_dimension=0, tiled=True)  142 us
    unnamed x2, blocking collectives  80.2 us
    all_gather x1, waiting for transfers between devices, body(): lax.all_gather(qkv_weight, ('seq', 'slot'), axis=0, tiled=True)  65.6 us
    all_gather x1, waiting for transfers between devices, body(): lax.all_gather(up_weight, ('seq', 'slot'), axis=0, tiled=True)  62.9 us
    all_gather x1, waiting for transfers between devices, body(): lax.all_gather(down_weight, ('seq', 'slot'), axis=0, tiled=True)  53.1 us
    unnamed x147, local copies, waits for them, and re-layouts  50.9 us
  transfers between devices with their start and end apart: 12, of which 11 were waited for; matrix products, arithmetic and copies ran while one was open for 12% of the time, Pallas kernels for 0%

commit v1 on v0

--- a/solution.py
+++ b/solution.py
@@ -1,3 +1,4 @@
+import functools
 import jax
 import jax.numpy as jnp
 from jax import lax
@@ -6,6 +7,23 @@
 HEADS = 12
 NEG_FILL = -1e30
 EPSILON = 1e-05
+
+
+def scan_the_sector(x_part, mesh_ax):
+    oldest, part_next = (jax.lax.axis_size(mesh_ax), jax.lax.axis_index(mesh_ax))
+    local_next, b_next = (x_part, 1)
+    while b_next < oldest:
+        block_last = jax.lax.ppermute(
+            local_next, mesh_ax, [(nth, nth ^ b_next) for nth in range(oldest)]
+        )
+        built = jnp.concatenate([local_next, block_last], axis=0)
+        x_new = jnp.concatenate([block_last, local_next], axis=0)
+        local_next = jnp.where(part_next & b_next == 0, built, x_new)
+        b_next = 2 * b_next
+    return local_next
+
+
+outputs_connect = functools.partial(scan_the_sector, mesh_ax=("seq", "slot"))
 
 
 def norm_rows(resid, gain, shift):
@@ -162,7 +180,7 @@
     head_count = HEADS
     flat_rows = tokens.reshape(slot_count * row_count, model_width)
     attn_set = (
-        lax.all_gather(qkv_weight, ("seq", "slot"), axis=0, tiled=True),
+        outputs_connect(qkv_weight),
         lax.all_gather(out_weight, ("seq", "slot"), axis=0, tiled=True),
         lax.all_gather(query_bias, ("seq", "slot"), axis=0, tiled=True),
         lax.all_gather(value_bias, ("seq", "slot"), axis=0, tiled=True),

time: 1050 us -> 1130 us (1.076)
  waiting for transfers between devices: 718 us -> 796 us
    ppermute x0 -> x5, waiting for transfers between devices: none -> 73.3 us  [scan_the_sector(): jax.lax.ppermute(local_next, mesh_ax, [(nth, nth ^ b_next) for nth in ran...]
    reduce_scatter x1, waiting for transfers between devices: 32.7 us -> 100 us  [body(): lax.psum_scatter(d_out, ('seq', 'slot'), scatter_dimension=0, tiled=True)]
    all_gather x1, waiting for transfers between devices: 65.6 us -> 1.99 us  [body(): lax.all_gather(qkv_weight, ('seq', 'slot'), axis=0, tiled=True)]
    unnamed x147 -> x153, local copies, waits for them, and re-layouts: 50.9 us -> 44.3 us
  transfers between devices with their start and end apart: 12 -> 17, of which waited for: 11 -> 16; matrix products, arithmetic and copies ran while one was open for 12% -> 11% of each run, Pallas kernels for 0% -> 0%
where the time goes in v1:
time: 1130 us
  waiting for transfers between devices  796 us (70%)
  matrix products  98.1 us (9%)
  local copies, waits for them, and re-layouts  89.3 us (8%)
  blocking collectives  81.7 us (7%)
  other arithmetic  29.7 us (3%)
  between operations  15.6 us (1%)
    unnamed x15, waiting for transfers between devices  183 us
    reduce_scatter x1, waiting for transfers between devices, body(): lax.psum_scatter(d_down, ('seq', 'slot'), scatter_dimension=0, tiled=True)  142 us
    reduce_scatter x1, waiting for transfers between devices, body(): lax.psum_scatter(d_up, ('seq', 'slot'), scatter_dimension=0, tiled=True)  142 us
    reduce_scatter x1, waiting for transfers between devices, body(): lax.psum_scatter(d_out, ('seq', 'slot'), scatter_dimension=0, tiled=True)  100 us
    unnamed x2, blocking collectives  81.7 us
    ppermute x5, waiting for transfers between devices, scan_the_sector(): jax.lax.ppermute(local_next, mesh_ax, [(nth, nth ^ b_next) for nth in ran...  73.3 us
    all_gather x1, waiting for transfers between devices, body(): lax.all_gather(up_weight, ('seq', 'slot'), axis=0, tiled=True)  62.9 us
    all_gather x1, waiting for transfers between devices, body(): lax.all_gather(down_weight, ('seq', 'slot'), axis=0, tiled=True)  53 us
  transfers between devices with their start and end apart: 17, of which 16 were waited for; matrix products, arithmetic and copies ran while one was open for 11% of the time, Pallas kernels for 0%

profile of v1, /device:TPU:0, one launch (start us, length us, event | category | flops | bytes accessed | tf_op | source)
XLA Modules:
  0.0 1126.4 jit_solution(16234625292130371162)
XLA Ops:
  7.2 3.1 collective-permute-start
  10.3 3.3 collective-permute-done
  14.6 2.8 collective-permute-start.1
  17.5 9.5 collective-permute-done.1
  30.5 20.3 %collective-permute-done.3 = bf16[192,2304]{1,0:T(8,128)(2,1)S(1)} collective-permute-done((bf16[192,2304]{1,0:T(8,128)(2,1)S(1)}, bf16[192,2304]{1,0:T(8,128)(2,1)S(1)}, u32[]{:S(2)}, u32[]{:S(2)}) %collective-permute-start.3) | collective-permute-done | bytes 884768 | tf_op jit(solution)/shard_map/ppermute | solution.py:16
  52.8 38.5 %collective-permute-done.4 = bf16[384,2304]{1,0:T(8,128)(2,1)} collective-permute-done((bf16[384,2304]{1,0:T(8,128)(2,1)S(1)}, bf16[384,2304]{1,0:T(8,128)(2,1)}, u32[]{:S(2)}, u32[]{:S(2)}) %collective-permute-start.4) | collective-permute-done | bytes 1769504 | tf_op jit(solution)/shard_map/ppermute | solution.py:16
  91.4 3.2 convolution_bitcast_fusion.2
  99.2 40.2 %all-reduce.19 = (bf16[3072]{0:T(1024)(128)(2,1)S(1)}, bf16[768]{0:T(1024)(128)(2,1)S(1)}, bf16[768]{0:T(1024)(128)(2,1)S(1)}, bf16[768]{0:T(1024)(128)(2,1)S(1)...) all-reduce(bf16[3072]{0:T(1024)(128)(2,1)S(1)} %dynamic-update-slic, ...), channel_id=1, replica_groups=mesh['seq'=8,'slot'=4] {'seq','slot'}, use_global_device_ids=true, to_apply=%add.5 | all-reduce | flops 9216 | bytes 36864
  151.2 22.2 %while.50 = (s32[]{:T(128)}, f32[2,12,128]{2,1,0:T(8,128)S(1)}, f32[2,12,128]{2,1,0:T(8,128)S(1)}, s32[2]{0:T(128)S(1)}, s32[2]{0:T(128)}, /*index=5*/bf16[2,102...) while((s32[]{:T(128)}, f32[2,12,128]{2,1,0:T(8,128)S(1)}, ...), condition=%wide.region_3.4_spmd.clone, body=%wide.region_0.3_spmd.clone.sunk | while | flops 209207808 | bytes 17861824 | solution.py:83
  154.7 4.1 bitcast_reduce_fusion.2
  158.8 3.5 fusion.126
  165.8 4.1 bitcast_reduce_fusion.2
  169.9 3.5 fusion.126
  175.6 18.6 %while.51 = (s32[]{:T(128)}, f32[2,128,12,64]{1,3,2,0:T(8,128)}, s32[2]{0:T(128)}, bf16[2,1024,768]{1,2,0:T(8,128)(2,1)}, s32[2]{0:T(128)}, /*index=5*/bf16[2,10...) while((s32[]{:T(128)}, f32[2,128,12,64]{1,3,2,0:T(8,128)}, ...), condition=%wide.region_5.6_spmd.clone, body=%wide.region_4.5_spmd.clone.sunk | while | flops 407766528 | bytes 11421897 | solution.py:103
  177.5 2.1 constant_dynamic-slice_fusion.12
  180.9 3.8 fusion.131
  186.6 2.1 constant_dynamic-slice_fusion.12
  190.0 4.2 fusion.131
  195.9 36.0 %all-gather.11.cloned.1.call-done = bf16[768,768]{1,0:T(8,128)(2,1)} async-done(((bf16[24,768]{1,0:T(8,128)(2,1)}), bf16[768,768]{1,0:T(8,128)(2,1)}) %all-gather.11.cloned.1.call-update) | async-done | bytes 1179664 | tf_op jit(solution)/shard_map/all_gather | solution.py:184
  231.9 2.0 fusion.57
  234.2 62.9 %all-gather.13.cloned.1.call-done = bf16[768,3072]{1,0:T(8,128)(2,1)} async-done(((bf16[24,3072]{1,0:T(8,128)(2,1)}), bf16[768,3072]{1,0:T(8,128)(2,1)}) %all-gather.13.cloned.1.call-update) | async-done | bytes 4718608 | tf_op jit(solution)/shard_map/all_gather | solution.py:225
  297.2 11.5 %multiply_convert_fusion.1 = (bf16[256,3072]{1,0:T(8,128)(2,1)S(1)}, f32[256,3072]{1,0:T(8,128)}, f32[256,3072]{1,0:T(8,128)}) fusion(f32[3072]{0:T(1024)S(1)} %copy-done.44, bf16[768,3072]{1,0:T(8,128)(2,1)} %all-gather.13.cloned.1.call-done, f32[256,768]{1,0:T(8,128)S(1)} %get-tuple-element.609, f32[768]{0:T(1024)S(1)} %copy-done.32, ...), kind=kOutput, calls=%fused_computation.61 | convolution fusion | flops 1260847104 | bytes 13389824 | tf_op jit(solution)/shard_map/dot_general | solution.py:233
  308.7 53.0 %all-gather.15.cloned.1.call-done = bf16[3072,768]{1,0:T(8,128)(2,1)} async-done(((bf16[96,768]{1,0:T(8,128)(2,1)}), bf16[3072,768]{1,0:T(8,128)(2,1)}) %all-gather.15.cloned.1.call-update) | async-done | bytes 4718608 | tf_op jit(solution)/shard_map/all_gather | solution.py:226
  361.8 4.0 fusion.58
  368.8 2.7 convert_reduce_fusion
  371.6 2.3 multiply_reduce_fusion.1
  377.6 14.8 %while.52 = (s32[]{:T(128)}, f32[2,12,128]{2,1,0:T(8,128)S(1)}, s32[2]{0:T(128)S(1)}, s32[2]{0:T(128)}, bf16[2,1024,768]{1,2,0:T(8,128)(2,1)}, /*index=5*/bf16[2...) while((s32[]{:T(128)}, f32[2,12,128]{2,1,0:T(8,128)S(1)}, ...), condition=%wide.region_16.17_spmd.clone, body=%wide.region_14.16_spmd.clone.sunk | while | flops 408949248 | bytes 22874320 | solution.py:124
  378.9 2.1 constant_dynamic-slice_fusion.13
  382.8 2.2 multiply_reduce_fusion.7
  386.3 2.1 constant_dynamic-slice_fusion.13
  390.2 2.2 multiply_reduce_fusion.7
  392.4 38.2 %while.53 = (s32[]{:T(128)}, f32[2,128,12,64]{1,3,2,0:T(8,128)}, bf16[2,2,512,12,64]{2,4,3,1,0:T(8,128)(2,1)}, bf16[2,2,512,12,64]{2,4,3,1,0:T(8,128)(2,1)}, s32...) while((s32[]{:T(128)}, f32[2,128,12,64]{1,3,2,0:T(8,128)}, ...), condition=%wide.region_18.19_spmd.clone, body=%wide.region_17.18_spmd.clone.sunk | while | flops 1019610624 | bytes 108679776 | solution.py:158
  394.0 2.1 constant_dynamic-slice_fusion.14
  398.0 3.9 multiply_convert_fusion.3
  401.9 2.4 bitcast_dynamic-update-slice_fusion.7
  404.3 3.2 fusion.148
  407.6 3.9 bitcast_dynamic-update-slice_fusion.8
  412.8 2.1 constant_dynamic-slice_fusion.14
  416.8 3.9 multiply_convert_fusion.3
  420.7 2.5 bitcast_dynamic-update-slice_fusion.7
  423.2 3.4 fusion.148
  426.7 3.9 bitcast_dynamic-update-slice_fusion.8
  430.7 5.1 copy.69
  435.8 3.9 convert_element_type.152
  439.7 7.6 copy.74
  447.3 2.3 copy.84
  449.9 5.1 copy.71
  455.1 3.9 convert_element_type.155
  459.0 7.7 copy.76
  466.7 2.3 copy.86
  470.3 1.9 fusion.42
  472.3 5.2 fusion.51
  479.0 5.1 fusion.61
  485.9 8.3 reduce-scatter.19.cloned.1.call-done
  495.8 47.9 %reduce-scatter.21.cloned.1.call-done = bf16[128,1536]{1,0:T(8,128)(2,1)} async-done(((bf16[1024,1536]{1,0:T(8,128)(2,1)}), bf16[128,1536]{1,0:T(8,128)(2,1)}) %reduce-scatter.21.cloned.1.call-update) | async-done | bytes 393232
  545.4 3.9 convolution_bitcast_fusion.1
  549.3 8.0 copy.78
  558.2 41.5 %all-reduce.18 = (f32[768]{0:T(1024)S(1)}, f32[768]{0:T(1024)S(1)}, f32[768]{0:T(1024)S(1)}, f32[768]{0:T(1024)S(1)}, f32[768]{0:T(1024)S(1)}, /*index=5*/f32[30...) all-reduce(f32[768]{0:T(1024)S(1)} %reduce_sum.185, ...), channel_id=5, replica_groups=mesh['seq'=8,'slot'=4] {'seq','slot'}, use_global_device_ids=true, to_apply=%region_23.24.clone | all-reduce | flops 9216 | bytes 73728
  605.0 2.0 all-gather.17.cloned.1.call-done
  607.0 3.9 fusion.36
  610.9 100.3 %reduce-scatter.13.cloned.1.call-done = f32[24,768]{1,0:T(8,128)} async-done(((f32[768,768]{1,0:T(8,128)}), f32[24,768]{1,0:T(8,128)}) %reduce-scatter.13.cloned.1.call-update) | async-done | bytes 73744 | tf_op jit(solution)/shard_map/reduce_scatter | solution.py:327
  711.2 141.5 %reduce-scatter.15.cloned.1.call-done = f32[24,3072]{1,0:T(8,128)} async-done(((f32[768,3072]{1,0:T(8,128)}), f32[24,3072]{1,0:T(8,128)}) %reduce-scatter.15.cloned.1.call-update) | async-done | bytes 294928 | tf_op jit(solution)/shard_map/reduce_scatter | solution.py:335
  852.7 141.6 %reduce-scatter.17.cloned.1.call-done = f32[96,768]{1,0:T(8,128)} async-done(((f32[3072,768]{1,0:T(8,128)}), f32[96,768]{1,0:T(8,128)}) %reduce-scatter.17.cloned.1.call-update) | async-done | bytes 294928 | tf_op jit(solution)/shard_map/reduce_scatter | solution.py:336
  994.4 124.6 %reduce-scatter.23.cloned.1.call-done = f32[24,2304]{1,0:T(8,128)} async-done(((f32[768,2304]{1,0:T(8,128)}), f32[24,2304]{1,0:T(8,128)}) %reduce-scatter.23.cloned.1.call-update) | async-done | bytes 221200
  (323 shorter events, 68.6 us)
Async XLA Ops:
  7.2 144.0 %all-gather.9.cloned.1.call-start = ((), (), s32[]{:S(2)}) async-start(), calls=%async_computation.7 | async-start | bytes 3538944 | tf_op jit(solution)/shard_map/all_gather | solution.py:208
  7.2 6.4 collective-permute-start
  14.6 12.3 %collective-permute-start.1 = (bf16[48,2304]{1,0:T(8,128)(2,1)S(1)}, bf16[48,2304]{1,0:T(8,128)(2,1)S(1)}, u32[]{:S(2)}, u32[]{:S(2)}) collective-permute-start(bf16[48,2304]{1,0:T(8,128)(2,1)S(1)} %maximum_select_fusion.5), channel_id=1, source_target_pairs={{0,2},{1,3},{2,0},{3,1},{4,6},{5,7},{6,4},{7,5},{8,10},{9,11},{10,... | collective-permute-start | bytes 663560 | tf_op jit(solution)/shard_map/ppermute | solution.py:16
  27.0 1.9 collective-permute-start.2
  29.0 21.8 %collective-permute-start.3 = (bf16[192,2304]{1,0:T(8,128)(2,1)S(1)}, bf16[192,2304]{1,0:T(8,128)(2,1)S(1)}, u32[]{:S(2)}, u32[]{:S(2)}) collective-permute-start(bf16[192,2304]{1,0:T(8,128)(2,1)S(1)} %maximum_select_fusion.3), channel_id=1, source_target_pairs={{0,8},{1,9},{2,10},{3,11},{4,12},{5,13},{6,14},{7,15},{8,0},{9,1},... | collective-permute-start | bytes 2654216 | tf_op jit(solution)/shard_map/ppermute | solution.py:16
  51.3 40.0 %collective-permute-start.4 = (bf16[384,2304]{1,0:T(8,128)(2,1)S(1)}, bf16[384,2304]{1,0:T(8,128)(2,1)}, u32[]{:S(2)}, u32[]{:S(2)}) collective-permute-start(bf16[384,2304]{1,0:T(8,128)(2,1)S(1)} %maximum_select_fusion.2), channel_id=1, source_target_pairs={{0,16},{1,17},{2,18},{3,19},{4,20},{5,21},{6,22},{7,23},{8,24},{9,... | collective-permute-start | bytes 5308424 | tf_op jit(solution)/shard_map/ppermute | solution.py:16
  91.3 5.7 copy-start.51
  91.3 6.0 copy-start.52
  91.3 6.2 copy-start.53
  91.3 6.5 copy-start.54
  91.3 6.7 copy-start.55
  91.3 6.9 copy-start.56
  91.3 7.1 copy-start.57
  91.3 7.4 copy-start.58
  91.3 7.6 copy-start.59
  96.0 49.1 %copy-start.29 = (bf16[2,128,768]{2,1,0:T(8,128)(2,1)S(1)}, bf16[2,128,768]{2,1,0:T(8,128)(2,1)}, u32[]{:S(2)}) copy-start(bf16[2,128,768]{2,1,0:T(8,128)(2,1)} %param.39) | copy-start | bytes 1179652
  97.0 78.2 %all-gather.7.cloned.1.call-start = ((), (), s32[]{:S(2)}) async-start(), calls=%async_computation.6 | async-start | bytes 3538944 | tf_op jit(solution)/shard_map/all_gather | solution.py:209
  141.8 90.2 %all-gather.11.cloned.1.call-start = ((), (), s32[]{:S(2)}) async-start(), calls=%async_computation.8 | async-start | bytes 1216512 | tf_op jit(solution)/shard_map/all_gather | solution.py:184
  142.5 154.6 %all-gather.13.cloned.1.call-start = ((), (), s32[]{:S(2)}) async-start(), calls=%async_computation.9 | async-start | bytes 4866048 | tf_op jit(solution)/shard_map/all_gather | solution.py:225
  143.1 218.6 %all-gather.15.cloned.1.call-start = ((), (), s32[]{:S(2)}) async-start(), calls=%async_computation.10 | async-start | bytes 4866048 | tf_op jit(solution)/shard_map/all_gather | solution.py:226
  143.7 350.5 %reduce-scatter.19.cloned.1.call-start = ((), (), s32[]{:S(2)}) async-start(), calls=%async_computation.15 | async-start | bytes 3538944
  194.3 102.9 %copy-start.30 = (f32[768]{0:T(1024)S(1)}, f32[768]{0:T(1024)}, u32[]{:S(2)}) copy-start(f32[768]{0:T(1024)} %convert_element_type.134) | copy-start | bytes 9220
  194.3 102.9 %copy-start.32 = (f32[768]{0:T(1024)S(1)}, f32[768]{0:T(1024)}, u32[]{:S(2)}) copy-start(f32[768]{0:T(1024)} %convert_element_type.135) | copy-start | bytes 9220
  194.3 102.9 %copy-start.44 = (f32[3072]{0:T(1024)S(1)}, f32[3072]{0:T(1024)}, u32[]{:S(2)}) copy-start(f32[3072]{0:T(1024)} %convert_element_type.137) | copy-start | bytes 36868
  195.9 38.3 %copy-start.21 = (bf16[2,128,12,64]{1,0,3,2:T(2,128)(2,1)}, bf16[2,128,12,64]{1,0,3,2:T(2,128)(2,1)S(1)}, u32[]{:S(2)}) copy-start(bf16[2,128,12,64]{1,0,3,2:T(2,128)(2,1)S(1)} %copy.62) | copy-start | bytes 1179652
  233.9 140.0 %copy-start.7 = (f32[256,768]{1,0:T(8,128)}, f32[256,768]{1,0:T(8,128)S(1)}, u32[]{:S(2)}) copy-start(f32[256,768]{1,0:T(8,128)S(1)} %get-tuple-element.609) | copy-start | bytes 2359300
  233.9 140.0 %copy-start.35 = (f32[256]{0:T(256)}, f32[256]{0:T(256)S(1)}, u32[]{:S(2)}) copy-start(f32[256]{0:T(256)S(1)} %broadcast_multiply_fusion.1) | copy-start | bytes 3076
  234.2 139.8 %copy-start.42 = (f32[256]{0:T(256)}, f32[256]{0:T(256)S(1)}, u32[]{:S(2)}) copy-start(f32[256]{0:T(256)S(1)} %fusion.48) | copy-start | bytes 3076
  234.2 127.5 %copy-start.46 = (f32[768]{0:T(1024)S(1)}, f32[768]{0:T(1024)}, u32[]{:S(2)}) copy-start(f32[768]{0:T(1024)} %convert_element_type.139) | copy-start | bytes 9220
  308.7 57.1 %copy-start.13 = (bf16[256,3072]{1,0:T(8,128)(2,1)}, bf16[256,3072]{1,0:T(8,128)(2,1)S(1)}, u32[]{:S(2)}) copy-start(bf16[256,3072]{1,0:T(8,128)(2,1)S(1)} %get-tuple-element.593) | copy-start | bytes 4718596
  361.7 7.1 slice-start.2
  361.7 4.3 copy-start.6
  361.7 4.3 copy-start.34
  361.7 5.2 copy-start.37
  361.8 7.0 slice-start.3
  368.1 3.5 slice-start
  374.3 3.3 copy-start.15
  392.7 3.4 copy-start.3
  392.7 3.4 copy-start.16
  392.7 3.4 copy-start.60
  397.3 4.6 copy-start
  398.0 3.9 copy-start.26
  407.6 3.9 copy-start.4
  407.6 3.9 copy-start.17
  407.6 3.9 copy-start.61
  411.5 3.4 copy-start.3
  411.5 3.4 copy-start.16
  411.5 3.4 copy-start.60
  416.1 4.6 copy-start
  416.8 3.9 copy-start.26
  423.2 3.5 copy-start.1
  423.2 3.5 copy-start.27
  426.7 3.9 copy-start.4
  426.7 3.9 copy-start.17
  426.7 3.9 copy-start.61
  449.6 94.0 %reduce-scatter.21.cloned.1.call-start = ((), (), s32[]{:S(2)}) async-start(), calls=%async_computation.16 | async-start | bytes 3538944
  469.0 137.9 %all-gather.17.cloned.1.call-start = ((), (), s32[]{:S(2)}) async-start(), calls=%async_computation.11 | async-start | bytes 3649536 | tf_op jit(solution)/shard_map/all_gather | solution.py:244
  469.8 241.4 %reduce-scatter.13.cloned.1.call-start = ((), (), s32[]{:S(2)}) async-start(), calls=%async_computation.12 | async-start | bytes 2433024 | tf_op jit(solution)/shard_map/reduce_scatter | solution.py:327
  472.2 380.6 %reduce-scatter.15.cloned.1.call-start = ((), (), s32[]{:S(2)}) async-start(), calls=%async_computation.13 | async-start | bytes 9732096 | tf_op jit(solution)/shard_map/reduce_scatter | solution.py:335
  477.6 516.8 %reduce-scatter.17.cloned.1.call-start = ((), (), s32[]{:S(2)}) async-start(), calls=%async_computation.14 | async-start | bytes 9732096 | tf_op jit(solution)/shard_map/reduce_scatter | solution.py:336
  484.1 634.9 %reduce-scatter.23.cloned.1.call-start = ((), (), s32[]{:S(2)}) async-start(), calls=%async_computation.17 | async-start | bytes 7299072
  485.4 60.0 %copy-start.28 = (bf16[2,128,768]{2,1,0:T(8,128)(2,1)S(1)}, bf16[2,128,768]{2,1,0:T(8,128)(2,1)}, u32[]{:S(2)}) copy-start(bf16[2,128,768]{2,1,0:T(8,128)(2,1)} %param.24) | copy-start | bytes 1179652
  557.4 49.6 %copy-start.12 = (f32[256,768]{1,0:T(8,128)S(1)}, f32[256,768]{1,0:T(8,128)}, u32[]{:S(2)}) copy-start(f32[256,768]{1,0:T(8,128)} %copy-done.11) | copy-start | bytes 2359300
  557.4 49.6 %copy-start.50 = (f32[256]{0:T(256)S(1)}, f32[256]{0:T(256)}, u32[]{:S(2)}) copy-start(f32[256]{0:T(256)} %copy-done.49) | copy-start | bytes 3076
  (32 other events, 64.0 us)
Sparse Core Ops, SparseCore 0:
  97.1 33.9 all-gather.8
  141.9 33.1 all-gather.6
  177.9 53.9 all-gather.10
  234.6 62.5 all-gather.12
  299.8 61.8 all-gather.14
  449.8 44.3 reduce-scatter.18
  497.6 46.0 reduce-scatter.20
  546.5 60.4 all-gather.16
  612.8 98.3 reduce-scatter.12
  717.5 135.1 reduce-scatter.14
  859.2 135.0 reduce-scatter.16
  1000.5 118.4 reduce-scatter.22
